TPU v7x, 32 devices: a whole 2x2x4 slice. The times are simulated.
32 devices in a mesh: dp: 8 (over z, x), tensor: 4 (over y, core).
Axes of the slice: x: 2, y: 2, z: 4, core: 2. Of those that a mesh axis runs over, the one named last changes fastest.
Arguments:
- block_input: float32 [8192, 1536], P(('dp', 'tensor')), may hold values from -6 to 6
- cotangent: float32 [8192, 1536], P(('dp', 'tensor')), may hold values from -6 to 6
- norm_gain: float32 [1536], replicated, may hold values from 0.5 to 1.5
- gate_proj: bfloat16 [1536, 3072], P('dp', 'tensor'), may hold values from -0.15625 to 0.15625
- value_proj: bfloat16 [1536, 3072], P('dp', 'tensor'), may hold values from -0.15625 to 0.15625
- state_proj: bfloat16 [1536, 256], P('dp'), may hold values from -0.15625 to 0.15625
- step_proj: bfloat16 [1536, 48], P('dp', 'tensor'), may hold values from -0.15625 to 0.15625
- value_conv: float32 [4, 3072], P(None, 'tensor'), may hold values from -3 to 3
- value_conv_bias: float32 [3072], P('tensor'), may hold values from -3 to 3
- state_conv: float32 [4, 256], replicated, may hold values from -3 to 3
- state_conv_bias: float32 [256], replicated, may hold values from -3 to 3
- step_bias: float32 [48], P('tensor'), may hold values from -7 to -2.3
- decay_log: float32 [48], P('tensor'), may hold values from 0 to 2.77
- skip_gain: float32 [48], P('tensor'), may hold values from 0.5 to 2
- mixer_gain: float32 [3072], P('tensor'), may hold values from 0.5 to 1.5
- out_proj: bfloat16 [3072, 1536], P('tensor', 'dp'), may hold values from -0.109375 to 0.109375
Outputs:
- block_output: float32 [8192, 1536], P(('dp', 'tensor'))
- input_grad: float32 [8192, 1536], P(('dp', 'tensor'))
- norm_gain_grad: float32 [1536], replicated
- gate_proj_grad: float32 [1536, 3072], P('dp', 'tensor')
- value_proj_grad: float32 [1536, 3072], P('dp', 'tensor')
- state_proj_grad: float32 [1536, 256], P('dp')
- step_proj_grad: float32 [1536, 48], P('dp', 'tensor')
- value_conv_grad: float32 [4, 3072], P(None, 'tensor')
- value_conv_bias_grad: float32 [3072], P('tensor')
- state_conv_grad: float32 [4, 256], replicated
- state_conv_bias_grad: float32 [256], replicated
- step_bias_grad: float32 [48], P('tensor')
- decay_log_grad: float32 [48], P('tensor')
- skip_gain_grad: float32 [48], P('tensor')
- mixer_gain_grad: float32 [3072], P('tensor')
- out_proj_grad: float32 [3072, 1536], P('tensor', 'dp')
All inputs are finite; a program needn't handle non-finite values.
Results may differ from a plain program's by a relative error of at most 0.0088.
Values may be sent and summed in bfloat16 or wider, within the bound.
No kernel may reach another device: no remote copies, remote signals or barrier semaphores. Data moves between devices by JAX's collectives and lax.ppermute only.
A program may use at most 192 MiB of HBM per device.

v0:
```python
import jax
import jax.numpy as jnp
from jax import lax
from jax.sharding import PartitionSpec as P

INNER = 3072
HEADDIM = 64
NSTATE = 128
BLOCK_LEN = 256
SEQLEN = 1024
norm_eps = 1e-05
highest = lax.Precision.HIGHEST


def causal_conv(values, kernel, offset_bias, seq_len):
    rows_all, channels = values.shape
    seq_count = rows_all // seq_len
    taps_count = kernel.shape[0]
    shaped = values.reshape(seq_count, seq_len, channels)
    padded = jnp.pad(shaped, ((0, 0), (taps_count - 1, 0), (0, 0)))
    running = jnp.zeros_like(shaped) + offset_bias
    for offset in range(taps_count):
        running = running + padded[:, offset : offset + seq_len, :] * kernel[offset]
    return running.reshape(rows_all, channels)


def block_scan(inputs, b_rows, c_rows, steps_dt, rate, skip_term, seq_len, block_len):
    rows_all, heads_here, head_dim = inputs.shape
    state_dim = b_rows.shape[1]
    seq_count = rows_all // seq_len
    block_count = seq_len // block_len
    x_blocks = inputs.reshape(seq_count, block_count, block_len, heads_here, head_dim)
    b_blocks = b_rows.reshape(seq_count, block_count, block_len, state_dim)
    c_blocks = c_rows.reshape(seq_count, block_count, block_len, state_dim)
    dt_blocks = steps_dt.reshape(seq_count, block_count, block_len, heads_here)
    log_decay = jnp.cumsum(dt_blocks * rate, axis=2)
    block_end = log_decay[:, :, -1, :]
    position = jnp.arange(block_len)
    causal = (position[:, None] >= position[None, :])[None, None, :, :, None]
    gaps = log_decay[:, :, :, None, :] - log_decay[:, :, None, :, :]
    decay_mat = jnp.where(causal, jnp.exp(jnp.where(causal, gaps, 0.0)), 0.0)
    scores = jnp.einsum("scin,scjn->scij", c_blocks, b_blocks, precision=highest)
    mixing = scores[..., None] * decay_mat
    x_scaled = x_blocks * dt_blocks[..., None]
    y_inner = jnp.einsum("scijh,scjhp->scihp", mixing, x_scaled, precision=highest)
    to_end = jnp.exp(block_end[:, :, None, :] - log_decay)
    block_states = jnp.einsum(
        "scjn,scjhp->schnp", b_blocks, x_scaled * to_end[..., None], precision=highest
    )

    def advance(carried, pieces):
        piece_state, piece_end = pieces
        return (carried * jnp.exp(piece_end)[:, :, None, None] + piece_state, carried)

    start_state = jnp.zeros((seq_count, heads_here, state_dim, head_dim), jnp.float32)
    _, entering = lax.scan(
        advance, start_state, (jnp.moveaxis(block_states, 1, 0), jnp.moveaxis(block_end, 1, 0))
    )
    entering = jnp.moveaxis(entering, 0, 1)
    y_outer = (
        jnp.einsum("scin,schnp->scihp", c_blocks, entering, precision=highest)
        * jnp.exp(log_decay)[..., None]
    )
    result = y_inner + y_outer + x_blocks * skip_term[:, None]
    return result.reshape(rows_all, heads_here, head_dim)


def mixer(
    gate_pre,
    value_pre,
    state_pre,
    step_pre,
    value_conv,
    value_conv_bias,
    state_conv,
    state_conv_bias,
    step_bias,
    decay_log,
    skip_gain,
):
    x_conv = jax.nn.silu(causal_conv(value_pre, value_conv, value_conv_bias, SEQLEN))
    bc_conv = jax.nn.silu(causal_conv(state_pre, state_conv, state_conv_bias, SEQLEN))
    steps_dt = jax.nn.softplus(step_pre + step_bias)
    rows_all = x_conv.shape[0]
    scanned = block_scan(
        x_conv.reshape(rows_all, -1, HEADDIM),
        bc_conv[:, :NSTATE],
        bc_conv[:, NSTATE:],
        steps_dt,
        -jnp.exp(decay_log),
        skip_gain,
        SEQLEN,
        BLOCK_LEN,
    )
    return scanned.reshape(rows_all, -1) * jax.nn.silu(gate_pre)


def contract_rows(left, right):
    return lax.dot_general(
        left, right, (((0,), (0,)), ((), ())), preferred_element_type=jnp.float32
    )


def contract_cols(left, right):
    return lax.dot_general(
        left, right, (((1,), (1,)), ((), ())), preferred_element_type=jnp.float32
    )


def shards(
    block_input,
    cotangent,
    norm_gain,
    gate_proj,
    value_proj,
    state_proj,
    step_proj,
    value_conv,
    value_conv_bias,
    state_conv,
    state_conv_bias,
    step_bias,
    decay_log,
    skip_gain,
    mixer_gain,
    out_proj,
):
    rms_inv = lax.rsqrt(jnp.mean(block_input * block_input, axis=1, keepdims=True) + norm_eps)
    normed = (block_input * rms_inv * norm_gain).astype(jnp.bfloat16)
    gathered = lax.all_gather(normed, "tensor", axis=0, tiled=True)
    gate_full, value_full, state_full, step_full, out_full = (
        lax.all_gather(gate_proj, "dp", axis=0, tiled=True),
        lax.all_gather(value_proj, "dp", axis=0, tiled=True),
        lax.all_gather(state_proj, "dp", axis=0, tiled=True),
        lax.all_gather(step_proj, "dp", axis=0, tiled=True),
        lax.all_gather(out_proj, "dp", axis=1, tiled=True),
    )
    gate_pre = jnp.dot(gathered, gate_full, preferred_element_type=jnp.float32)
    value_pre = jnp.dot(gathered, value_full, preferred_element_type=jnp.float32)
    state_pre = jnp.dot(gathered, state_full, preferred_element_type=jnp.float32)
    step_pre = jnp.dot(gathered, step_full, preferred_element_type=jnp.float32)
    gated, pull_back = jax.vjp(
        mixer,
        gate_pre,
        value_pre,
        state_pre,
        step_pre,
        value_conv,
        value_conv_bias,
        state_conv,
        state_conv_bias,
        step_bias,
        decay_log,
        skip_gain,
    )
    row_squares = lax.psum(jnp.sum(gated * gated, axis=1, keepdims=True), "tensor")
    gate_inv = lax.rsqrt(row_squares / INNER + norm_eps)
    mixed_rows = (gated * gate_inv * mixer_gain).astype(jnp.bfloat16)
    block_output = block_input + lax.psum_scatter(
        jnp.dot(mixed_rows, out_full, preferred_element_type=jnp.float32),
        "tensor",
        scatter_dimension=0,
        tiled=True,
    )
    cot_low = cotangent.astype(jnp.bfloat16)
    cot_full = lax.all_gather(cot_low, "tensor", axis=0, tiled=True)
    mixed_grad = contract_cols(cot_full, out_full)
    gain_term = jnp.sum(mixed_grad * gated * gate_inv, axis=0)
    scaled_grad = mixed_grad * mixer_gain
    row_dot = lax.psum(jnp.sum(scaled_grad * gated, axis=1, keepdims=True), "tensor")
    gated_grad = gate_inv * scaled_grad - gated * gate_inv**3 * row_dot / INNER
    pulled = pull_back(gated_grad)
    state_total = lax.psum(pulled[2], "tensor")
    gate_low = pulled[0].astype(jnp.bfloat16)
    value_low = pulled[1].astype(jnp.bfloat16)
    state_low = state_total.astype(jnp.bfloat16)
    step_low = pulled[3].astype(jnp.bfloat16)
    first_flag = (lax.axis_index("tensor") == 0).astype(jnp.float32)
    running = (
        contract_cols(gate_low, gate_full)
        + contract_cols(value_low, value_full)
        + contract_cols(step_low, step_full)
    )
    normed_grad = lax.psum_scatter(
        running + first_flag * contract_cols(state_low, state_full),
        "tensor",
        scatter_dimension=0,
        tiled=True,
    )
    norm_term = jnp.sum(normed_grad * block_input * rms_inv, axis=0)
    scaled_in = normed_grad * norm_gain
    input_grad = (
        rms_inv * scaled_in
        - block_input * rms_inv**3 * jnp.mean(scaled_in * block_input, axis=1, keepdims=True)
        + cotangent
    )
    out_grad = contract_rows(mixed_rows, cot_full)
    proj_sums = (
        lax.psum_scatter(contract_rows(gathered, gate_low), "dp", scatter_dimension=0, tiled=True),
        lax.psum_scatter(contract_rows(gathered, value_low), "dp", scatter_dimension=0, tiled=True),
        lax.psum_scatter(contract_rows(gathered, state_low), "dp", scatter_dimension=0, tiled=True),
        lax.psum_scatter(contract_rows(gathered, step_low), "dp", scatter_dimension=0, tiled=True),
        lax.psum_scatter(out_grad, "dp", scatter_dimension=1, tiled=True),
    )
    gate_grad, value_grad, state_grad, step_grad, out_grad_owned = proj_sums
    small_sums = lax.psum((pulled[4], pulled[5], pulled[8], pulled[9], pulled[10], gain_term), "dp")
    shared_sums = lax.psum((norm_term, pulled[6], pulled[7]), ("dp", "tensor"))
    return (
        block_output,
        input_grad,
        shared_sums[0],
        gate_grad,
        value_grad,
        state_grad,
        step_grad,
        small_sums[0],
        small_sums[1],
        shared_sums[1],
        shared_sums[2],
        small_sums[2],
        small_sums[3],
        small_sums[4],
        small_sums[5],
        out_grad_owned,
    )


def solution(mesh):
    in_specs = (
        P(("dp", "tensor"), None),
        P(("dp", "tensor"), None),
        P(),
        P("dp", "tensor"),
        P("dp", "tensor"),
        P("dp", None),
        P("dp", "tensor"),
        P(None, "tensor"),
        P("tensor"),
        P(),
        P(),
        P("tensor"),
        P("tensor"),
        P("tensor"),
        P("tensor"),
        P("tensor", "dp"),
    )
    out_specs = (
        P(("dp", "tensor"), None),
        P(("dp", "tensor"), None),
        P(),
        P("dp", "tensor"),
        P("dp", "tensor"),
        P("dp", None),
        P("dp", "tensor"),
        P(None, "tensor"),
        P("tensor"),
        P(),
        P(),
        P("tensor"),
        P("tensor"),
        P("tensor"),
        P("tensor"),
        P("tensor", "dp"),
    )
    return jax.shard_map(shards, mesh=mesh, in_specs=in_specs, out_specs=out_specs, check_vma=False)
```

profile of v0, /device:TPU:0, one launch (start us, length us, event | category | flops | bytes accessed | tf_op | source)
XLA Modules:
  0.0 941.6 jit_solution(11002507970807550462)
XLA Ops:
  16.6 32.4 %all-gather = bf16[8,192,12]{1,2,0:T(8,128)(2,1)S(1)} all-gather(bf16[1,192,12]{1,2,0:T(8,128)(2,1)S(1)} %bitcast.399), channel_id=1, replica_groups=mesh['dp'=8,'tensor'=4] {'dp'}, dimensions={0}, use_global_device_ids=true | all-gather | bytes 41472 | tf_op jit(solution)/shard_map/all_gather | solution.py:135
  49.1 33.3 %all_gather.24 = bf16[1536,256]{1,0:T(8,128)(2,1)S(1)} all-gather(bf16[192,256]{1,0:T(8,128)(2,1)S(1)} %copy-done.34), channel_id=1, replica_groups=mesh['dp'=8,'tensor'=4] {'dp'}, dimensions={0}, use_global_device_ids=true | all-gather | bytes 884736 | tf_op jit(solution)/shard_map/all_gather | solution.py:134
  82.4 3.7 compare_select_fusion.2
  96.0 6.1 all-gather.9.cloned.1.call-done
  102.1 5.2 fusion.125
  115.8 5.1 reshape.652
  121.0 6.8 fusion.63
  130.4 13.9 %while.36 = (s32[]{:T(128)}, f32[1,12,128,64]{3,2,1,0:T(8,128)S(1)}, f32[4,1,12,128,64]{4,3,2,1,0:T(8,128)}, f32[4,1,12]{2,1,0:T(1,128)}, f32[4,1,12,1,1]{2,4,3,...) while((s32[]{:T(128)}, ...), condition=%wide.region_4.5_spmd.clone, body=%wide.region_3.4_spmd.clone.sunk | while | flops 393219 | bytes 3933504 | solution.py:56
  144.3 5.2 reshape.664
  149.6 3.7 copy.390
  159.1 16.4 %fusion.33 = f32[1,4,256,12,64]{2,4,3,1,0:T(8,128)S(1)} fusion(f32[4,256,12,64]{1,3,2,0:T(8,128)S(1)} %bitcast.363, f32[4,256,12]{1,2,0:T(8,128)S(1)} %copy.382, f32[4,256,256]{2,1,0:T(8,128)S(1)} %fusion.127, pred[256,256]{1,0:T(8,128)(4,1)S(1)} %copy-done.43, f32[12]{0:T(128)S(1)} %copy-done.67, f32[4,256,12]{1,2,0:T(8,128)S(1)} %copy.391, ...), kind=kOutput, calls=%fused_computation.59 | convolution fusion | flops 2438725632 | bytes 13844528 | tf_op jit(solution)/shard_map/jvp(scijh,scjhp->scihp)/dot_general | solution.py:45
  183.5 9.2 multiply_reduce_fusion.7
  192.8 6.0 psum.84
  198.8 9.4 all-gather.13.cloned.1.call-done
  208.2 29.1 %all-gather.15.cloned.1.call-done = bf16[1024,1536]{1,0:T(8,128)(2,1)} async-done(((bf16[256,1536]{1,0:T(8,128)(2,1)}), bf16[1024,1536]{1,0:T(8,128)(2,1)}) %all-gather.15.cloned.1.call-update) | async-done | bytes 3145744 | tf_op jit(solution)/shard_map/all_gather | solution.py:166
  237.3 8.0 multiply_reduce_fusion
  245.2 5.9 psum.85
  251.1 7.3 fusion.25
  262.0 5.1 reshape.667
  267.1 5.4 reshape.666
  272.5 3.9 multiply_reduce_fusion.4
  277.2 10.9 %fusion.66 = f32[4,256,128]{2,1,0:T(8,128)} fusion(f32[4,256,12,64]{1,0,3,2:T(4,128)S(1)} %copy-done.1, f32[4,256,12]{1,2,0:T(8,128)S(1)} %copy.391, f32[4,1,12,128,64]{4,3,2,1,0:T(8,128)S(1)} %copy-done), kind=kOutput, calls=%fused_computation.120 | convolution fusion | flops 1208745984 | bytes 5292032 | tf_op jit(solution)/shard_map/transpose(jvp(scin,schnp->scihp))/dot_general | solution.py:61
  288.1 4.7 fusion.62
  294.8 20.0 %while.37 = (s32[]{:T(128)}, f32[1,12,128,64]{3,2,1,0:T(8,128)S(1)}, f32[4,1,12,128,64]{4,3,2,1,0:T(8,128)}, f32[4,1,12]{2,1,0:T(1,128)S(1)}, f32[4,1,12,128,64]...) while((s32[]{:T(128)}, ...), condition=%wide.region_12.13_spmd.clone, body=%wide.region_10.12_spmd.clone.sunk | while | flops 589828 | bytes 4326800 | solution.py:56
  314.7 21.2 %fusion.12 = (f32[4,256,12]{1,2,0:T(8,128)S(1)}, f32[4,256,12]{1,2,0:T(8,128)S(1)}, f32[4,256,256]{2,1,0:T(8,128)S(1)}) fusion(f32[4,256,12]{1,2,0:T(8,128)S(1)} %copy.382, f32[4,256,256]{2,1,0:T(8,128)} %copy-done.30, pred[256,256]{1,0:T(8,128)(4,1)S(1)} %copy-done.43, f32[4,256,12,64]{1,0,3,2:T(4,128)} %reshape.652, f32[4,256,12]{1,2,0:T(8,128)S(1)} %copy-done.37, ...), kind=kOutput, calls=%fused_computation.29 | convolution fusion | flops 2454167552 | bytes 8650752 | tf_op jit(solution)/shard_map/transpose(jvp(scijh,scjhp->scihp))/dot_general | solution.py:45
  337.1 5.1 fusion.41
  342.3 3.8 fusion.72
  346.2 13.9 %fusion.43 = (f32[4,256,12]{1,2,0:T(8,128)S(1)}, f32[4,256,12]{1,2,0:T(8,128)S(1)}, f32[1,4,256,12,64]{2,4,3,1,0:T(8,128)}) fusion(f32[4,12,64,256]{3,2,1,0:T(8,128)S(1)} %fusion.41, f32[4,256,12]{1,2,0:T(8,128)S(1)} %copy-done.38, f32[1,4,256,12,64]{2,1,4,3,0:T(4,128)S(1)} %copy-done.22, f32[12]{0:T(128)S(1)} %copy-done.67, ...), kind=kOutput, calls=%fused_computation.74 | convolution fusion | flops 2439487488 | bytes 17088560 | tf_op jit(solution)/shard_map/transpose(jvp(scijh,scjhp->scihp))/dot_general | solution.py:45
  363.6 9.9 %reduce-window.16 = f32[1,4,12,2,128]{4,2,3,1,0:T(8,128)S(1)} reduce-window(f32[1,4,12,2,128]{4,2,3,1,0:T(8,128)S(1)} %copy.421, f32[]{:T(128)} %constant.104.clone.1), window={size=1x1x1x1x128 pad=0_0x0_0x0_0x0_0x0_127}, to_apply=%region_19.20 | reduce-window | flops 1560576 | bytes 98308 | tf_op jit(solution)/shard_map/reduce-window.2
  380.1 3.9 copy.407
  389.0 3.7 copy.408
  392.8 5.7 multiply_reduce_fusion.3
  401.7 26.7 %all-reduce.24 = bf16[1024,256]{1,0:T(8,128)(2,1)} all-reduce(f32[1024,256]{1,0:T(8,128)} %fusion.79), channel_id=1, replica_groups=mesh['dp'=8,'tensor'=4] {'tensor'}, use_global_device_ids=true, to_apply=%region_22.23 | all-reduce | flops 262144 | bytes 1572864 | tf_op jit(solution)/shard_map/psum | solution.py:173
  439.4 3.9 multiply_add_fusion
  443.6 7.9 fusion.115
  451.6 4.6 fusion.133
  456.2 8.3 fusion.114
  464.7 7.2 fusion.131
  472.1 7.2 fusion.132
  479.4 4.4 copy.449
  487.3 4.7 fusion.38
  492.3 37.9 %all-reduce.22 = (f32[4,768]{1,0:T(4,128)}, f32[768]{0:T(1024)}, f32[12]{0:T(128)}, f32[12]{0:T(128)}, f32[12]{0:T(128)}, /*index=5*/f32[768]{0:T(1024)}) all-reduce(f32[4,768]{1,0:T(4,128)S(1)} %pad_add_fusion.6, f32[768]{0:T(1024)S(1)} %get-tuple-element.387, ...), channel_id=1, replica_groups=mesh['dp'=8,'tensor'=4] {'dp'}, use_global_device_ids=true, to_apply=%region_35.36 | all-reduce | flops 4644 | bytes 37152 | tf_op jit(solution)/shard_map/psum | solution.py:206
  536.6 37.8 %all-reduce.21 = (f32[1536]{0:T(1024)}, f32[4,256]{1,0:T(4,128)}, f32[256]{0:T(256)}) all-reduce(f32[1536]{0:T(1024)S(1)} %get-tuple-element.388, f32[4,256]{1,0:T(4,128)S(1)} %pad_add_fusion.7, f32[256]{0:T(256)S(1)} %get-tuple-element.395), channel_id=1, replica_groups=mesh['dp'=8,'tensor'=4] {'dp','tensor'}, use_global_device_ids=true, to_apply=%region_26.27 | all-reduce | flops 2816 | bytes 22528 | tf_op jit(solution)/shard_map/psum | solution.py:207
  574.3 4.0 subtract_add_fusion
  578.3 58.5 %reduce-scatter.18.cloned.1.call-done = f32[192,256]{1,0:T(8,128)} async-done(((f32[1536,256]{1,0:T(8,128)}), f32[192,256]{1,0:T(8,128)}) %reduce-scatter.18.cloned.1.call-update) | async-done | bytes 196624 | tf_op jit(solution)/shard_map/reduce_scatter | solution.py:201
  636.8 98.6 %reduce-scatter.20.cloned.1.call-done = f32[768,192]{0,1:T(8,128)} async-done(((f32[768,1536]{0,1:T(8,128)}), f32[768,192]{0,1:T(8,128)}) %reduce-scatter.20.cloned.1.call-update) | async-done | bytes 589840 | tf_op jit(solution)/shard_map/reduce_scatter | solution.py:203
  735.4 99.6 %reduce-scatter.14.cloned.1.call-done = f32[192,768]{1,0:T(8,128)} async-done(((f32[1536,768]{1,0:T(8,128)}), f32[192,768]{1,0:T(8,128)}) %reduce-scatter.14.cloned.1.call-update) | async-done | bytes 589840 | tf_op jit(solution)/shard_map/reduce_scatter | solution.py:199
  835.0 99.4 %reduce-scatter.16.cloned.1.call-done = f32[192,768]{1,0:T(8,128)} async-done(((f32[1536,768]{1,0:T(8,128)}), f32[192,768]{1,0:T(8,128)}) %reduce-scatter.16.cloned.1.call-update) | async-done | bytes 589840 | tf_op jit(solution)/shard_map/reduce_scatter | solution.py:200
  (321 shorter events, 124.6 us)
Async XLA Ops:
  7.2 7.6 copy-start.14
  7.2 75.2 %all-gather.7.cloned.1.call-start = ((), (), s32[]{:S(2)}) async-start(), calls=%async_computation.7 | async-start | bytes 3932160 | tf_op jit(solution)/shard_map/all_gather | solution.py:130
  10.1 6.4 copy-start.68
  10.1 6.4 copy-start.60
  10.1 6.4 copy-start.47
  10.1 6.5 copy-start.56
  12.6 36.5 %copy-start.34 = (bf16[192,256]{1,0:T(8,128)(2,1)S(1)}, bf16[192,256]{1,0:T(8,128)(2,1)}, u32[]{:S(2)}) copy-start(bf16[192,256]{1,0:T(8,128)(2,1)} %param.25) | copy-start | bytes 294916
  12.6 69.8 %copy-start.63 = (f32[12]{0:T(128)S(1)}, f32[12]{0:T(128)}, u32[]{:S(2)}) copy-start(f32[12]{0:T(128)} %param.31) | copy-start | bytes 148
  12.6 89.5 %all-gather.9.cloned.1.call-start = ((), (), s32[]{:S(2)}) async-start(), calls=%async_computation.8 | async-start | bytes 2654208 | tf_op jit(solution)/shard_map/all_gather | solution.py:133
  13.4 170.1 %all-gather.11.cloned.1.call-start = ((), (), s32[]{:S(2)}) async-start(), calls=%async_computation.9 | async-start | bytes 2654208 | tf_op jit(solution)/shard_map/all_gather | solution.py:132
  14.1 194.1 %all-gather.13.cloned.1.call-start = ((), (), s32[]{:S(2)}) async-start(), calls=%async_computation.10 | async-start | bytes 2654208 | tf_op jit(solution)/shard_map/all_gather | solution.py:136
  14.7 222.6 %all-gather.15.cloned.1.call-start = ((), (), s32[]{:S(2)}) async-start(), calls=%async_computation.12 | async-start | bytes 3932160 | tf_op jit(solution)/shard_map/all_gather | solution.py:166
  15.7 517.4 %reduce-scatter.22.cloned.1.call-start = ((), (), s32[]{:S(2)}) async-start(), calls=%async_computation.18 | async-start | bytes 884736
  16.5 69.8 %copy-start.61 = (f32[12]{0:T(128)}, f32[12]{0:T(128)S(1)}, u32[]{:S(2)}) copy-start(f32[12]{0:T(128)S(1)} %exponential_negate_fusion) | copy-start | bytes 148
  16.5 76.8 %copy-start.48 = (f32[1,256]{1,0:T(1,128)}, f32[1,256]{1,0:T(1,128)S(1)}, u32[]{:S(2)}) copy-start(f32[1,256]{1,0:T(1,128)S(1)} %get-tuple-element.473) | copy-start | bytes 3076
  16.5 76.8 %copy-start.50 = (f32[1,256]{1,0:T(1,128)}, f32[1,256]{1,0:T(1,128)S(1)}, u32[]{:S(2)}) copy-start(f32[1,256]{1,0:T(1,128)S(1)} %get-tuple-element.474) | copy-start | bytes 3076
  16.5 76.8 %copy-start.52 = (f32[1,256]{1,0:T(1,128)}, f32[1,256]{1,0:T(1,128)S(1)}, u32[]{:S(2)}) copy-start(f32[1,256]{1,0:T(1,128)S(1)} %get-tuple-element.475) | copy-start | bytes 3076
  16.6 76.8 %copy-start.54 = (f32[1,256]{1,0:T(1,128)}, f32[1,256]{1,0:T(1,128)S(1)}, u32[]{:S(2)}) copy-start(f32[1,256]{1,0:T(1,128)S(1)} %get-tuple-element.476) | copy-start | bytes 3076
  82.4 7.9 copy-start.18
  88.8 32.1 %copy-start.36 = (f32[4,256,12]{1,2,0:T(8,128)}, f32[4,256,12]{1,2,0:T(8,128)S(1)}, u32[]{:S(2)}) copy-start(f32[4,256,12]{1,2,0:T(8,128)S(1)} %copy.375) | copy-start | bytes 147460
  90.4 30.6 %copy-start.39 = (f32[4,256,12]{1,2,0:T(8,128)}, f32[4,256,12]{1,2,0:T(8,128)S(1)}, u32[]{:S(2)}) copy-start(f32[4,256,12]{1,2,0:T(8,128)S(1)} %copy.387) | copy-start | bytes 147460
  96.0 25.0 %copy-start.12 = (f32[1024,128]{1,0:T(8,128)}, f32[1024,128]{1,0:T(8,128)S(1)}, u32[]{:S(2)}) copy-start(f32[1024,128]{1,0:T(8,128)S(1)} %get-tuple-element.469) | copy-start | bytes 1572868
  96.0 13.0 %copy-start.57 = (f32[768]{0:T(1024)S(1)}, f32[768]{0:T(1024)}, u32[]{:S(2)}) copy-start(f32[768]{0:T(1024)} %param.28) | copy-start | bytes 9220
  144.3 5.2 copy-start.33
  149.6 165.1 %copy-start.41 = (f32[4,256,12]{1,2,0:T(8,128)}, f32[4,256,12]{1,2,0:T(8,128)S(1)}, u32[]{:S(2)}) copy-start(f32[4,256,12]{1,2,0:T(8,128)S(1)} %copy.382) | copy-start | bytes 147460
  154.4 21.1 %copy-start.30 = (f32[4,256,256]{2,1,0:T(8,128)}, f32[4,256,256]{2,1,0:T(8,128)S(1)}, u32[]{:S(2)}) copy-start(f32[4,256,256]{2,1,0:T(8,128)S(1)} %fusion.127) | copy-start | bytes 3145732
  183.5 53.8 %copy-start.58 = (f32[768]{0:T(1024)S(1)}, f32[768]{0:T(1024)}, u32[]{:S(2)}) copy-start(f32[768]{0:T(1024)} %param.34) | copy-start | bytes 9220
  314.7 22.3 %copy-start.10 = (f32[4,1,12,128,64]{4,3,2,1,0:T(8,128)S(1)}, f32[4,1,12,128,64]{4,3,2,1,0:T(8,128)}, u32[]{:S(2)}) copy-start(f32[4,1,12,128,64]{4,3,2,1,0:T(8,128)} %get-tuple-element.219) | copy-start | bytes 4718596
  337.1 5.2 copy-start.21
  346.2 14.9 %copy-start.25 = (f32[4,256,128]{2,1,0:T(8,128)S(1)}, f32[4,256,128]{2,1,0:T(8,128)}, u32[]{:S(2)}) copy-start(f32[4,256,128]{2,1,0:T(8,128)} %fusion.66) | copy-start | bytes 1572868
  360.1 13.9 %copy-start.62 = (f32[12]{0:T(128)S(1)}, f32[12]{0:T(128)}, u32[]{:S(2)}) copy-start(f32[12]{0:T(128)} %copy-done.61) | copy-start | bytes 148
  360.1 14.1 %copy-start.32 = (f32[1024,12]{0,1:T(8,128)S(1)}, f32[1024,12]{0,1:T(8,128)}, u32[]{:S(2)}) copy-start(f32[1024,12]{0,1:T(8,128)} %get-tuple-element.480) | copy-start | bytes 147460
  380.0 154.7 %reduce-scatter.12.cloned.1.call-start = ((), (), s32[]{:S(2)}) async-start(), calls=%async_computation.13 | async-start | bytes 7864320 | tf_op jit(solution)/shard_map/reduce_scatter | solution.py:184
  392.8 5.8 copy-start.8
  392.8 5.8 copy-start.17
  392.8 5.8 copy-start.26
  392.8 5.8 copy-start.27
  434.0 5.3 slice-start
  443.4 131.0 %reduce-scatter.10.cloned.1.call-start = ((), (), s32[]{:S(2)}) async-start(), calls=%async_computation.11 | async-start | bytes 7864320 | tf_op jit(solution)/shard_map/reduce_scatter | solution.py:159
  451.5 185.3 %reduce-scatter.18.cloned.1.call-start = ((), (), s32[]{:S(2)}) async-start(), calls=%async_computation.16 | async-start | bytes 1769472 | tf_op jit(solution)/shard_map/reduce_scatter | solution.py:201
  456.2 279.3 %reduce-scatter.20.cloned.1.call-start = ((), (), s32[]{:S(2)}) async-start(), calls=%async_computation.17 | async-start | bytes 5308416 | tf_op jit(solution)/shard_map/reduce_scatter | solution.py:203
  464.6 370.4 %reduce-scatter.14.cloned.1.call-start = ((), (), s32[]{:S(2)}) async-start(), calls=%async_computation.14 | async-start | bytes 5308416 | tf_op jit(solution)/shard_map/reduce_scatter | solution.py:199
  471.9 462.6 %reduce-scatter.16.cloned.1.call-start = ((), (), s32[]{:S(2)}) async-start(), calls=%async_computation.15 | async-start | bytes 5308416 | tf_op jit(solution)/shard_map/reduce_scatter | solution.py:200
  487.3 47.5 %copy-start.35 = (f32[1536]{0:T(1024)S(1)}, f32[1536]{0:T(1024)}, u32[]{:S(2)}) copy-start(f32[1536]{0:T(1024)} %param.22) | copy-start | bytes 18436
  487.3 47.5 %copy-start.46 = (f32[256]{0:T(256)S(1)}, f32[256]{0:T(256)}, u32[]{:S(2)}) copy-start(f32[256]{0:T(256)} %copy-done.45) | copy-start | bytes 3076
  492.0 42.7 %copy-start.6 = (f32[256,1536]{1,0:T(8,128)S(1)}, f32[256,1536]{1,0:T(8,128)}, u32[]{:S(2)}) copy-start(f32[256,1536]{1,0:T(8,128)} %param.20) | copy-start | bytes 4718596
  492.1 82.3 %copy-start.15 = (f32[256,1536]{1,0:T(8,128)S(1)}, f32[256,1536]{1,0:T(8,128)}, u32[]{:S(2)}) copy-start(f32[256,1536]{1,0:T(8,128)} %param.21) | copy-start | bytes 4718596
  492.1 82.3 %copy-start.59 = (f32[256]{0:T(256)S(1)}, f32[256]{0:T(256)}, u32[]{:S(2)}) copy-start(f32[256]{0:T(256)} %get-tuple-element.477) | copy-start | bytes 3076
  (36 other events, 111.2 us)
Sparse Core Ops, SparseCore 0:
  12.8 31.2 all-gather.6
  46.2 55.8 all-gather.8
  104.3 51.6 all-gather.10
  158.0 50.1 all-gather.12
  210.2 27.0 all-gather.14
  380.1 64.2 reduce-scatter.21
  447.0 57.9 reduce-scatter.11
  507.5 59.6 reduce-scatter.9
  571.2 65.6 reduce-scatter.17
  640.9 94.5 reduce-scatter.19
  739.7 95.3 reduce-scatter.13
  839.1 95.3 reduce-scatter.15
where the time goes:
time: 953 us; the launch traced here: 942 us
  waiting for transfers between devices  403 us (42%)
  blocking collectives  180 us (19%)
  matrix products  169 us (18%)
  local copies, waits for them, and re-layouts  95.7 us (10%)
  other arithmetic  77.9 us (8%)
  between operations  15.6 us (2%)
    reduce_scatter x1, waiting for transfers between devices, shards(): lax.psum_scatter(contract_rows(gathered, gate_low), 'dp', scatter_dimensi...  99.6 us
    reduce_scatter x1, waiting for transfers between devices, shards(): lax.psum_scatter(contract_rows(gathered, value_low), 'dp', scatter_dimens...  99.4 us
    reduce_scatter x1, waiting for transfers between devices, shards(): lax.psum_scatter(out_grad, 'dp', scatter_dimension=1, tiled=True)  98.6 us
    reduce_scatter x1, waiting for transfers between devices, shards(): lax.psum_scatter(contract_rows(gathered, state_low), 'dp', scatter_dimens...  58.5 us
    dot_general x3, matrix products, block_scan(): jnp.einsum('scijh,scjhp->scihp', mixing, x_scaled, precision=highest)  51.6 us
    psum x1, blocking collectives, shards(): lax.psum((pulled[4], pulled[5], pulled[8], pulled[9], pulled[10], gain_te...  37.9 us
    psum x1, blocking collectives, shards(): shared_sums = lax.psum((norm_term, pulled[6], pulled[7]), ('dp', 'tensor'))  37.8 us
    all_gather x1, blocking collectives, shards(): lax.all_gather(state_proj, 'dp', axis=0, tiled=True)  33.3 us
  transfers between devices with their start and end apart: 12, of which 7 were waited for; matrix products, arithmetic and copies ran while one was open for 20% of the time, Pallas kernels for 0%

commit v1 on v0

--- a/solution.py
+++ b/solution.py
@@ -170,7 +170,7 @@
     row_dot = lax.psum(jnp.sum(scaled_grad * gated, axis=1, keepdims=True), "tensor")
     gated_grad = gate_inv * scaled_grad - gated * gate_inv**3 * row_dot / INNER
     pulled = pull_back(gated_grad)
-    state_total = lax.psum(pulled[2], "tensor")
+    state_total = jnp.sum(lax.all_gather(pulled[2], "tensor"), axis=0)
     gate_low = pulled[0].astype(jnp.bfloat16)
     value_low = pulled[1].astype(jnp.bfloat16)
     state_low = state_total.astype(jnp.bfloat16)

time: 953 us -> 991 us (1.040)
  waiting for transfers between devices: 403 us -> 437 us
  blocking collectives: 180 us -> 156 us
  matrix products: 169 us -> 187 us
  other arithmetic: 77.9 us -> 89.5 us
    psum x1 -> x0, blocking collectives: 26.7 us -> none  [shards(): state_total = lax.psum(pulled[2], 'tensor')]
    reduce_scatter x1, waiting for transfers between devices: 0.01 us -> 20.2 us  [shards(): lax.psum_scatter(jnp.dot(mixed_rows, out_full, preferred_element_type=jnp...]
    dot_general x5, matrix products: 20.8 us -> 32.1 us  [contract_cols(): lax.dot_general(left, right, (((1,), (1,)), ((), ())), preferred_element_...]
    reduce_scatter x1, waiting for transfers between devices: 58.5 us -> 69 us  [shards(): lax.psum_scatter(contract_rows(gathered, state_low), 'dp', scatter_dimens...]
  transfers between devices with their start and end apart: 12 -> 13, of which waited for: 7 -> 9; matrix products, arithmetic and copies ran while one was open for 20% -> 26% of each run, Pallas kernels for 0% -> 0%
where the time goes in v1:
time: 991 us; the launch traced here: 980 us
  waiting for transfers between devices  437 us (44%)
  matrix products  187 us (19%)
  blocking collectives  156 us (16%)
  local copies, waits for them, and re-layouts  94.6 us (10%)
  other arithmetic  89.5 us (9%)
  between operations  15.6 us (2%)
    reduce_scatter x1, waiting for transfers between devices, shards(): lax.psum_scatter(contract_rows(gathered, gate_low), 'dp', scatter_dimensi...  99.6 us
    reduce_scatter x1, waiting for transfers between devices, shards(): lax.psum_scatter(contract_rows(gathered, value_low), 'dp', scatter_dimens...  98.7 us
    reduce_scatter x1, waiting for transfers between devices, shards(): lax.psum_scatter(out_grad, 'dp', scatter_dimension=1, tiled=True)  95.3 us
    reduce_scatter x1, waiting for transfers between devices, shards(): lax.psum_scatter(contract_rows(gathered, state_low), 'dp', scatter_dimens...  69 us
    dot_general x3, matrix products, block_scan(): jnp.einsum('scijh,scjhp->scihp', mixing, x_scaled, precision=highest)  52.7 us
    psum x1, blocking collectives, shards(): shared_sums = lax.psum((norm_term, pulled[6], pulled[7]), ('dp', 'tensor'))  40.1 us
    psum x1, blocking collectives, shards(): lax.psum((pulled[4], pulled[5], pulled[8], pulled[9], pulled[10], gain_te...  37.9 us
    all_gather x1, blocking collectives, shards(): lax.all_gather(state_proj, 'dp', axis=0, tiled=True)  33.4 us
  transfers between devices with their start and end apart: 13, of which 9 were waited for; matrix products, arithmetic and copies ran while one was open for 26% of the time, Pallas kernels for 0%

profile of v1, /device:TPU:0, one launch (start us, length us, event | category | flops | bytes accessed | tf_op | source)
XLA Modules:
  0.0 979.7 jit_solution(4446598101532636848)
XLA Ops:
  16.1 32.4 %all-gather = bf16[8,192,12]{1,2,0:T(8,128)(2,1)S(1)} all-gather(bf16[1,192,12]{1,2,0:T(8,128)(2,1)S(1)} %bitcast.395), channel_id=1, replica_groups=mesh['dp'=8,'tensor'=4] {'dp'}, dimensions={0}, use_global_device_ids=true | all-gather | bytes 41472 | tf_op jit(solution)/shard_map/all_gather | solution.py:135
  48.6 33.4 %all_gather.27 = bf16[1536,256]{1,0:T(8,128)(2,1)S(1)} all-gather(bf16[192,256]{1,0:T(8,128)(2,1)S(1)} %copy-done.33), channel_id=1, replica_groups=mesh['dp'=8,'tensor'=4] {'dp'}, dimensions={0}, use_global_device_ids=true | all-gather | bytes 884736 | tf_op jit(solution)/shard_map/all_gather | solution.py:134
  95.6 6.0 all-gather.10.cloned.1.call-done
  101.7 5.2 fusion.124
  115.2 5.1 reshape.649
  120.4 6.8 fusion.63
  129.2 11.9 %while.36 = (s32[]{:T(128)}, f32[1,12,128,64]{3,2,1,0:T(8,128)S(1)}, f32[4,1,12,128,64]{4,3,2,1,0:T(8,128)}, f32[4,1,12]{2,1,0:T(1,128)S(1)}, f32[4,1,12,1,1]{2,...) while((s32[]{:T(128)}, ...), condition=%wide.region_4.5_spmd.clone, body=%wide.region_3.4_spmd.clone.sunk | while | flops 393219 | bytes 3934432 | solution.py:56
  141.1 5.3 reshape.661
  155.8 16.7 %fusion.33 = f32[1,4,256,12,64]{2,4,3,1,0:T(8,128)S(1)} fusion(f32[4,256,12,64]{1,3,2,0:T(8,128)S(1)} %bitcast.359, f32[4,256,12]{1,2,0:T(8,128)S(1)} %copy.382, f32[4,256,256]{2,1,0:T(8,128)S(1)} %fusion.126, pred[256,256]{1,0:T(8,128)(4,1)S(1)} %copy-done.43, f32[12]{0:T(128)S(1)} %copy-done.86, f32[4,256,12]{1,2,0:T(8,128)S(1)} %copy.391, ...), kind=kOutput, calls=%fused_computation.59 | convolution fusion | flops 2438725632 | bytes 13844528 | tf_op jit(solution)/shard_map/jvp(scijh,scjhp->scihp)/dot_general | solution.py:45
  180.4 9.3 multiply_reduce_fusion.7
  189.7 6.0 psum.77
  195.8 12.0 %all-gather.14.cloned.1.call-done = bf16[768,1536]{0,1:T(8,128)(2,1)} async-done(((bf16[768,192]{0,1:T(8,128)(2,1)}), bf16[768,1536]{0,1:T(8,128)(2,1)}) %all-gather.14.cloned.1.call-update) | async-done | bytes 2359312 | tf_op jit(solution)/shard_map/all_gather | solution.py:136
  207.8 29.1 %all-gather.16.cloned.1.call-done = bf16[1024,1536]{1,0:T(8,128)(2,1)} async-done(((bf16[256,1536]{1,0:T(8,128)(2,1)}), bf16[1024,1536]{1,0:T(8,128)(2,1)}) %all-gather.16.cloned.1.call-update) | async-done | bytes 3145744 | tf_op jit(solution)/shard_map/all_gather | solution.py:166
  236.9 8.5 multiply_reduce_fusion
  245.4 5.9 psum.78
  251.3 7.2 fusion.25
  262.1 5.2 reshape.664
  267.2 5.3 reshape.663
  272.5 13.9 %fusion.66 = f32[4,256,128]{2,1,0:T(8,128)} fusion(f32[4,256,12,64]{1,0,3,2:T(4,128)} %reshape.664, f32[4,256,12]{1,2,0:T(8,128)S(1)} %copy.391, f32[4,1,12,128,64]{4,3,2,1,0:T(8,128)} %get-tuple-element.618), kind=kOutput, calls=%fused_computation.120 | convolution fusion | flops 1208745984 | bytes 5292032 | tf_op jit(solution)/shard_map/transpose(jvp(scin,schnp->scihp))/dot_general | solution.py:61
  286.4 4.5 fusion.62
  292.9 19.9 %while.37 = (s32[]{:T(128)}, f32[1,12,128,64]{3,2,1,0:T(8,128)S(1)}, f32[4,1,12,128,64]{4,3,2,1,0:T(8,128)}, f32[4,1,12]{2,1,0:T(1,128)S(1)}, f32[4,1,12,128,64]...) while((s32[]{:T(128)}, ...), condition=%wide.region_12.13_spmd.clone, body=%wide.region_10.12_spmd.clone.sunk | while | flops 589828 | bytes 4326800 | solution.py:56
  313.3 22.1 %fusion.12 = (f32[4,256,12]{1,2,0:T(8,128)S(1)}, f32[4,256,12]{1,2,0:T(8,128)}, f32[4,256,256]{2,1,0:T(8,128)S(1)}) fusion(f32[4,256,12]{1,2,0:T(8,128)S(1)} %copy.382, f32[4,256,256]{2,1,0:T(8,128)} %copy-done.25, pred[256,256]{1,0:T(8,128)(4,1)S(1)} %copy-done.43, f32[4,256,12,64]{1,0,3,2:T(4,128)} %reshape.649, f32[4,256,12]{1,2,0:T(8,128)S(1)} %copy-done.36, ...), kind=kOutput, calls=%fused_computation.29 | convolution fusion | flops 2454167552 | bytes 8650752 | tf_op jit(solution)/shard_map/transpose(jvp(scijh,scjhp->scihp))/dot_general | solution.py:45
  336.6 4.6 fusion.72
  349.4 7.2 fusion.41
  356.8 13.9 %fusion.43 = (f32[4,256,12]{1,2,0:T(8,128)S(1)}, f32[4,256,12]{1,2,0:T(8,128)S(1)}, f32[1,4,256,12,64]{2,4,3,1,0:T(8,128)}) fusion(f32[4,12,64,256]{3,2,1,0:T(8,128)S(1)} %fusion.41, f32[4,256,12]{1,2,0:T(8,128)S(1)} %copy-done.37, f32[1,4,256,12,64]{2,1,4,3,0:T(4,128)S(1)} %copy-done.20, f32[12]{0:T(128)S(1)} %copy-done.87, ...), kind=kOutput, calls=%fused_computation.74 | convolution fusion | flops 2439487488 | bytes 17088560 | tf_op jit(solution)/shard_map/transpose(jvp(scijh,scjhp->scihp))/dot_general | solution.py:45
  375.1 9.9 %reduce-window.16 = f32[1,4,12,2,128]{4,2,3,1,0:T(8,128)S(1)} reduce-window(f32[1,4,12,2,128]{4,2,3,1,0:T(8,128)S(1)} %copy.421, f32[]{:T(128)} %constant.104.clone.1), window={size=1x1x1x1x128 pad=0_0x0_0x0_0x0_0x0_127}, to_apply=%region_19.20 | reduce-window | flops 1560576 | bytes 98308 | tf_op jit(solution)/shard_map/reduce-window.2
  386.3 5.6 copy.407
  391.9 5.3 reshape.667
  413.8 4.7 broadcast_multiply_fusion
  418.6 5.8 fusion.56
  424.4 4.6 fusion.128
  429.0 4.5 fusion.129
  436.1 10.4 %multiply_add_fusion = f32[1024,1536]{1,0:T(8,128)} fusion(f32[1024,1536]{1,0:T(8,128)} %fusion.101, f32[1024,1536]{1,0:T(8,128)} %fusion.128, f32[1024,1536]{1,0:T(8,128)} %fusion.129, bf16[1536,256]{1,0:T(8,128)(2,1)S(1)} %copy-done.17, f32[]{:T(128)S(6)} %convert_element_type.35, bf16[1024,256]{1,0:T(8,128)(2,1)S(1)} %reduce_sum.282), kind=kOutput, calls=%fused_computation.30 | convolution fusion | flops 811597824 | bytes 26476548 | tf_op jit(solution)/shard_map/dot_general | solution.py:105
  447.2 7.9 fusion.114
  455.2 7.8 fusion.113
  463.3 7.2 fusion.130
  474.7 7.2 fusion.131
  481.9 4.3 copy.449
  489.9 7.5 fusion.38
  497.6 37.9 %all-reduce.22 = (f32[4,768]{1,0:T(4,128)}, f32[768]{0:T(1024)}, f32[12]{0:T(128)}, f32[12]{0:T(128)}, f32[12]{0:T(128)}, /*index=5*/f32[768]{0:T(1024)}) all-reduce(f32[4,768]{1,0:T(4,128)S(1)} %pad_add_fusion.6, f32[768]{0:T(1024)S(1)} %get-tuple-element.387, ...), channel_id=1, replica_groups=mesh['dp'=8,'tensor'=4] {'dp'}, use_global_device_ids=true, to_apply=%region_35.36 | all-reduce | flops 4644 | bytes 37152 | tf_op jit(solution)/shard_map/psum | solution.py:206
  538.8 4.6 reduce-scatter.12.cloned.1.call-done
  545.3 40.1 %all-reduce.21 = (f32[1536]{0:T(1024)}, f32[4,256]{1,0:T(4,128)}, f32[256]{0:T(256)}) all-reduce(f32[1536]{0:T(1024)S(1)} %get-tuple-element.388, f32[4,256]{1,0:T(4,128)S(1)} %pad_add_fusion.7, f32[256]{0:T(256)S(1)} %copy-done.77), channel_id=1, replica_groups=mesh['dp'=8,'tensor'=4] {'dp','tensor'}, use_global_device_ids=true, to_apply=%region_26.27 | all-reduce | flops 2816 | bytes 22528 | tf_op jit(solution)/shard_map/psum | solution.py:207
  585.4 20.2 %reduce-scatter.10.cloned.1.call-done = f32[256,1536]{1,0:T(8,128)} async-done(((f32[1024,1536]{1,0:T(8,128)}), f32[256,1536]{1,0:T(8,128)}) %reduce-scatter.10.cloned.1.call-update) | async-done | bytes 1572880 | tf_op jit(solution)/shard_map/reduce_scatter | solution.py:159
  605.6 4.5 subtract_add_fusion
  610.0 95.3 %reduce-scatter.20.cloned.1.call-done = f32[768,192]{0,1:T(8,128)} async-done(((f32[768,1536]{0,1:T(8,128)}), f32[768,192]{0,1:T(8,128)}) %reduce-scatter.20.cloned.1.call-update) | async-done | bytes 589840 | tf_op jit(solution)/shard_map/reduce_scatter | solution.py:203
  705.3 99.6 %reduce-scatter.14.cloned.1.call-done = f32[192,768]{1,0:T(8,128)} async-done(((f32[1536,768]{1,0:T(8,128)}), f32[192,768]{1,0:T(8,128)}) %reduce-scatter.14.cloned.1.call-update) | async-done | bytes 589840 | tf_op jit(solution)/shard_map/reduce_scatter | solution.py:199
  804.9 69.0 %reduce-scatter.18.cloned.1.call-done = f32[192,256]{1,0:T(8,128)} async-done(((f32[1536,256]{1,0:T(8,128)}), f32[192,256]{1,0:T(8,128)}) %reduce-scatter.18.cloned.1.call-update) | async-done | bytes 196624 | tf_op jit(solution)/shard_map/reduce_scatter | solution.py:201
  873.9 98.7 %reduce-scatter.16.cloned.1.call-done = f32[192,768]{1,0:T(8,128)} async-done(((f32[1536,768]{1,0:T(8,128)}), f32[192,768]{1,0:T(8,128)}) %reduce-scatter.16.cloned.1.call-update) | async-done | bytes 589840 | tf_op jit(solution)/shard_map/reduce_scatter | solution.py:200
  (359 shorter events, 135.9 us)
Async XLA Ops:
  7.2 74.8 %all-gather.8.cloned.1.call-start = ((), (), s32[]{:S(2)}) async-start(), calls=%async_computation.7 | async-start | bytes 3932160 | tf_op jit(solution)/shard_map/all_gather | solution.py:130
  12.0 36.5 %copy-start.33 = (bf16[192,256]{1,0:T(8,128)(2,1)S(1)}, bf16[192,256]{1,0:T(8,128)(2,1)}, u32[]{:S(2)}) copy-start(bf16[192,256]{1,0:T(8,128)(2,1)} %param.25) | copy-start | bytes 294916
  12.0 69.9 %copy-start.81 = (f32[12]{0:T(128)S(1)}, f32[12]{0:T(128)}, u32[]{:S(2)}) copy-start(f32[12]{0:T(128)} %param.31) | copy-start | bytes 148
  12.1 89.6 %all-gather.10.cloned.1.call-start = ((), (), s32[]{:S(2)}) async-start(), calls=%async_computation.8 | async-start | bytes 2654208 | tf_op jit(solution)/shard_map/all_gather | solution.py:133
  12.8 167.6 %all-gather.12.cloned.1.call-start = ((), (), s32[]{:S(2)}) async-start(), calls=%async_computation.9 | async-start | bytes 2654208 | tf_op jit(solution)/shard_map/all_gather | solution.py:132
  13.6 194.3 %all-gather.14.cloned.1.call-start = ((), (), s32[]{:S(2)}) async-start(), calls=%async_computation.10 | async-start | bytes 2654208 | tf_op jit(solution)/shard_map/all_gather | solution.py:136
  14.1 222.7 %all-gather.16.cloned.1.call-start = ((), (), s32[]{:S(2)}) async-start(), calls=%async_computation.12 | async-start | bytes 3932160 | tf_op jit(solution)/shard_map/all_gather | solution.py:166
  15.2 418.3 %all-gather.18.cloned.1.call-start = ((), (), s32[]{:S(2)}) async-start(), calls=%async_computation.13 | async-start | bytes 5242880 | tf_op jit(solution)/shard_map/all_gather | solution.py:173
  15.9 69.9 %copy-start.79 = (f32[12]{0:T(128)}, f32[12]{0:T(128)S(1)}, u32[]{:S(2)}) copy-start(f32[12]{0:T(128)S(1)} %exponential_negate_fusion) | copy-start | bytes 148
  15.9 76.9 %copy-start.60 = (f32[1,256]{1,0:T(1,128)}, f32[1,256]{1,0:T(1,128)S(1)}, u32[]{:S(2)}) copy-start(f32[1,256]{1,0:T(1,128)S(1)} %get-tuple-element.473) | copy-start | bytes 3076
  16.0 76.9 %copy-start.62 = (f32[1,256]{1,0:T(1,128)}, f32[1,256]{1,0:T(1,128)S(1)}, u32[]{:S(2)}) copy-start(f32[1,256]{1,0:T(1,128)S(1)} %get-tuple-element.474) | copy-start | bytes 3076
  16.0 76.9 %copy-start.64 = (f32[1,256]{1,0:T(1,128)}, f32[1,256]{1,0:T(1,128)S(1)}, u32[]{:S(2)}) copy-start(f32[1,256]{1,0:T(1,128)S(1)} %get-tuple-element.475) | copy-start | bytes 3076
  16.0 76.9 %copy-start.66 = (f32[1,256]{1,0:T(1,128)}, f32[1,256]{1,0:T(1,128)S(1)}, u32[]{:S(2)}) copy-start(f32[1,256]{1,0:T(1,128)S(1)} %get-tuple-element.476) | copy-start | bytes 3076
  16.0 90.9 %copy-start.46 = (f32[768]{0:T(1024)}, f32[768]{0:T(1024)S(1)}, u32[]{:S(2)}) copy-start(f32[768]{0:T(1024)S(1)} %get-tuple-element.397) | copy-start | bytes 9220
  16.0 90.9 %copy-start.48 = (f32[768]{0:T(1024)}, f32[768]{0:T(1024)S(1)}, u32[]{:S(2)}) copy-start(f32[768]{0:T(1024)S(1)} %get-tuple-element.398) | copy-start | bytes 9220
  16.1 90.9 %copy-start.50 = (f32[768]{0:T(1024)}, f32[768]{0:T(1024)S(1)}, u32[]{:S(2)}) copy-start(f32[768]{0:T(1024)S(1)} %get-tuple-element.399) | copy-start | bytes 9220
  16.1 90.8 %copy-start.52 = (f32[768]{0:T(1024)}, f32[768]{0:T(1024)S(1)}, u32[]{:S(2)}) copy-start(f32[768]{0:T(1024)S(1)} %get-tuple-element.400) | copy-start | bytes 9220
  82.0 7.9 copy-start.16
  88.4 32.0 %copy-start.35 = (f32[4,256,12]{1,2,0:T(8,128)}, f32[4,256,12]{1,2,0:T(8,128)S(1)}, u32[]{:S(2)}) copy-start(f32[4,256,12]{1,2,0:T(8,128)S(1)} %copy.375) | copy-start | bytes 147460
  89.9 30.4 %copy-start.38 = (f32[4,256,12]{1,2,0:T(8,128)}, f32[4,256,12]{1,2,0:T(8,128)S(1)}, u32[]{:S(2)}) copy-start(f32[4,256,12]{1,2,0:T(8,128)S(1)} %copy.387) | copy-start | bytes 147460
  95.6 24.8 %copy-start.10 = (f32[1024,128]{1,0:T(8,128)}, f32[1024,128]{1,0:T(8,128)S(1)}, u32[]{:S(2)}) copy-start(f32[1024,128]{1,0:T(8,128)S(1)} %get-tuple-element.469) | copy-start | bytes 1572868
  95.6 12.9 %copy-start.71 = (f32[768]{0:T(1024)S(1)}, f32[768]{0:T(1024)}, u32[]{:S(2)}) copy-start(f32[768]{0:T(1024)} %param.28) | copy-start | bytes 9220
  146.5 166.9 %copy-start.41 = (f32[4,256,12]{1,2,0:T(8,128)}, f32[4,256,12]{1,2,0:T(8,128)S(1)}, u32[]{:S(2)}) copy-start(f32[4,256,12]{1,2,0:T(8,128)S(1)} %copy.382) | copy-start | bytes 147460
  151.0 21.4 %copy-start.25 = (f32[4,256,256]{2,1,0:T(8,128)}, f32[4,256,256]{2,1,0:T(8,128)S(1)}, u32[]{:S(2)}) copy-start(f32[4,256,256]{2,1,0:T(8,128)S(1)} %fusion.126) | copy-start | bytes 3145732
  180.4 56.5 %copy-start.72 = (f32[768]{0:T(1024)S(1)}, f32[768]{0:T(1024)}, u32[]{:S(2)}) copy-start(f32[768]{0:T(1024)} %param.34) | copy-start | bytes 9220
  195.8 55.5 %copy-start.56 = (f32[1024,1]{0,1:T(1,128)}, f32[1024,1]{0,1:T(1,128)S(1)}, u32[]{:S(2)}) copy-start(f32[1024,1]{0,1:T(1,128)S(1)} %get-tuple-element.445) | copy-start | bytes 12292
  272.5 13.9 %copy-start = (f32[4,256,12,64]{1,0,3,2:T(4,128)S(1)}, f32[4,256,12,64]{1,0,3,2:T(4,128)}, u32[]{:S(2)}) copy-start(f32[4,256,12,64]{1,0,3,2:T(4,128)} %reshape.664) | copy-start | bytes 9437188
  313.3 23.2 %copy-start.8 = (f32[4,1,12,128,64]{4,3,2,1,0:T(8,128)S(1)}, f32[4,1,12,128,64]{4,3,2,1,0:T(8,128)}, u32[]{:S(2)}) copy-start(f32[4,1,12,128,64]{4,3,2,1,0:T(8,128)} %get-tuple-element.219) | copy-start | bytes 4718596
  313.3 23.2 %copy-start.19 = (f32[4,256,12,64]{1,0,3,2:T(4,128)S(1)}, f32[4,256,12,64]{1,0,3,2:T(4,128)}, u32[]{:S(2)}) copy-start(f32[4,256,12,64]{1,0,3,2:T(4,128)} %reshape.649) | copy-start | bytes 9437188
  313.3 23.2 %copy-start.39 = (f32[4,256,12]{1,2,0:T(8,128)S(1)}, f32[4,256,12]{1,2,0:T(8,128)}, u32[]{:S(2)}) copy-start(f32[4,256,12]{1,2,0:T(8,128)} %copy-done.38) | copy-start | bytes 147460
  349.3 188.0 %reduce-scatter.22.cloned.1.call-start = ((), (), s32[]{:S(2)}) async-start(), calls=%async_computation.19 | async-start | bytes 884736
  356.8 13.9 %copy-start.32 = (f32[4,12]{0,1:T(8,128)S(1)}, f32[4,12]{0,1:T(8,128)}, u32[]{:S(2)}) copy-start(f32[4,12]{0,1:T(8,128)} %copy-done.31) | copy-start | bytes 580
  356.8 14.2 %copy-start.70 = (f32[4,1,12]{2,1,0:T(1,128)S(1)}, f32[4,1,12]{2,1,0:T(1,128)}, u32[]{:S(2)}) copy-start(f32[4,1,12]{2,1,0:T(1,128)} %copy-done.69) | copy-start | bytes 580
  371.1 14.5 %copy-start.80 = (f32[12]{0:T(128)S(1)}, f32[12]{0:T(128)}, u32[]{:S(2)}) copy-start(f32[12]{0:T(128)} %copy-done.79) | copy-start | bytes 148
  418.5 124.9 %reduce-scatter.12.cloned.1.call-start = ((), (), s32[]{:S(2)}) async-start(), calls=%async_computation.14 | async-start | bytes 7864320 | tf_op jit(solution)/shard_map/reduce_scatter | solution.py:184
  446.5 159.0 %reduce-scatter.10.cloned.1.call-start = ((), (), s32[]{:S(2)}) async-start(), calls=%async_computation.11 | async-start | bytes 7864320 | tf_op jit(solution)/shard_map/reduce_scatter | solution.py:159
  455.1 250.2 %reduce-scatter.20.cloned.1.call-start = ((), (), s32[]{:S(2)}) async-start(), calls=%async_computation.18 | async-start | bytes 5308416 | tf_op jit(solution)/shard_map/reduce_scatter | solution.py:203
  463.0 341.9 %reduce-scatter.14.cloned.1.call-start = ((), (), s32[]{:S(2)}) async-start(), calls=%async_computation.15 | async-start | bytes 5308416 | tf_op jit(solution)/shard_map/reduce_scatter | solution.py:199
  470.5 403.5 %reduce-scatter.18.cloned.1.call-start = ((), (), s32[]{:S(2)}) async-start(), calls=%async_computation.17 | async-start | bytes 1769472 | tf_op jit(solution)/shard_map/reduce_scatter | solution.py:201
  474.6 498.0 %reduce-scatter.16.cloned.1.call-start = ((), (), s32[]{:S(2)}) async-start(), calls=%async_computation.16 | async-start | bytes 5308416 | tf_op jit(solution)/shard_map/reduce_scatter | solution.py:200
  489.8 7.8 copy-start.89
  489.8 7.8 copy-start.76
  489.8 47.4 %copy-start.78 = (f32[256]{0:T(256)S(1)}, f32[256]{0:T(256)}, u32[]{:S(2)}) copy-start(f32[256]{0:T(256)} %get-tuple-element.396) | copy-start | bytes 3076
  489.8 53.6 %copy-start.34 = (f32[1536]{0:T(1024)S(1)}, f32[1536]{0:T(1024)}, u32[]{:S(2)}) copy-start(f32[1536]{0:T(1024)} %param.22) | copy-start | bytes 18436
  489.9 53.6 %copy-start.55 = (f32[256]{0:T(256)S(1)}, f32[256]{0:T(256)}, u32[]{:S(2)}) copy-start(f32[256]{0:T(256)} %copy-done.54) | copy-start | bytes 3076
  497.3 46.1 %copy-start.4 = (f32[256,1536]{1,0:T(8,128)S(1)}, f32[256,1536]{1,0:T(8,128)}, u32[]{:S(2)}) copy-start(f32[256,1536]{1,0:T(8,128)} %param.20) | copy-start | bytes 4718596
  497.3 47.9 %copy-start.77 = (f32[256]{0:T(256)S(1)}, f32[256]{0:T(256)}, u32[]{:S(2)}) copy-start(f32[256]{0:T(256)} %get-tuple-element.395) | copy-start | bytes 3076
  497.4 108.2 %copy-start.74 = (f32[256]{0:T(256)S(1)}, f32[256]{0:T(256)}, u32[]{:S(2)}) copy-start(f32[256]{0:T(256)} %get-tuple-element.477) | copy-start | bytes 3076
  (55 other events, 254.6 us)
Sparse Core Ops, SparseCore 0:
  12.2 31.2 all-gather.7
  45.6 55.9 all-gather.9
  103.8 51.5 all-gather.11
  157.4 50.3 all-gather.13
  209.8 27.0 all-gather.15
  349.4 35.5 all-gather.17
  418.6 64.2 reduce-scatter.21
  485.5 57.9 reduce-scatter.11
  546.0 59.5 reduce-scatter.9
  609.6 95.6 reduce-scatter.19
  709.5 95.3 reduce-scatter.13
  808.8 65.1 reduce-scatter.17
  878.2 94.4 reduce-scatter.15
